TPU v7x, 32 devices: a whole 2x2x4 slice. The times are simulated.
32 devices in a mesh: dp: 4 (over y, core), feat: 8 (over z, x).
Axes of the slice: x: 2, y: 2, z: 4, core: 2. Of those that a mesh axis runs over, the one named last changes fastest.
Arguments:
- images: bfloat16 [1536, 3072], P('dp'), may hold values from -6 to 6
- labels: int32 [1536], P('dp'), may hold values from 0 to 9
- frequencies: bfloat16 [3072, 8192], P(None, 'feat'), may hold values from -0.15625 to 0.15625
- privacy_noise: float32 [10, 2, 8192], P(None, None, 'feat'), may hold values from -0.6 to 0.6
- latents: bfloat16 [1024, 256], P('dp'), may hold values from -6 to 6
- gen_labels: int32 [1024], P('dp'), may hold values from 0 to 9
- gen_in: bfloat16 [256, 1024], replicated, may hold values from -0.375 to 0.375
- gen_out: bfloat16 [1024, 3072], replicated, may hold values from -0.25 to 0.25
Outputs:
- match_loss: float32 [], replicated
- grad_in: float32 [256, 1024], P('dp')
- grad_out: float32 [1024, 3072], P('dp')
All inputs are finite; a program needn't handle non-finite values.
Results may differ from a plain program's by a relative error of at most 0.0035.
Values sent between devices are 32-bit elements; how exact they have to be, the bound alone decides.
No kernel may reach another device: no remote copies, remote signals or barrier semaphores. Data moves between devices by JAX's collectives and lax.ppermute only.
A program may use at most 128 MiB of HBM per device.

v0:
```python
import jax
import jax.numpy as jnp
from jax import lax
from jax.sharding import PartitionSpec as P


def class_sums(phase, classes_of, classes, scale):
    feats = jnp.concatenate([jnp.cos(phase), jnp.sin(phase)], axis=1)
    onehot = (classes_of[:, None] == jnp.arange(classes)[None, :]).astype(jnp.float32)
    sums = jnp.dot(onehot.T, feats, precision=lax.Precision.HIGHEST) * scale
    return (sums.reshape(classes, 2, phase.shape[1]), onehot)


def generator_grads(image_grad, image_out, hidden, pre_hidden, sigmoid_h, latents, gen_out):
    out_grad = (image_grad * (1.0 - image_out * image_out)).astype(jnp.bfloat16)
    grad_out = jnp.einsum("gh,gd->hd", hidden, out_grad, preferred_element_type=jnp.float32)
    back_hidden = jnp.einsum("gd,hd->gh", out_grad, gen_out, preferred_element_type=jnp.float32)
    hidden_grad = (back_hidden * sigmoid_h * (1.0 + pre_hidden * (1.0 - sigmoid_h))).astype(
        jnp.bfloat16
    )
    grad_in = jnp.einsum("gz,gh->zh", latents, hidden_grad, preferred_element_type=jnp.float32)
    return (grad_in, grad_out)


def per_device(images, labels, frequencies, privacy_noise, latents, gen_labels, gen_in, gen_out):
    classes = privacy_noise.shape[0]
    feat_dev = frequencies.shape[1]
    data_devices = lax.axis_size("dp")
    feat_devices = lax.axis_size("feat")
    total_images = images.shape[0] * data_devices
    total_gen = latents.shape[0] * data_devices
    total_feats = feat_dev * feat_devices
    data_phase = jnp.dot(images, frequencies, preferred_element_type=jnp.float32)
    data_part, unused = class_sums(data_phase, labels, classes, classes / total_images)
    pre_hidden = jnp.dot(latents, gen_in, preferred_element_type=jnp.float32)
    sigmoid_h = jax.nn.sigmoid(pre_hidden)
    hidden = (pre_hidden * sigmoid_h).astype(jnp.bfloat16)
    image_out = jnp.tanh(jnp.dot(hidden, gen_out, preferred_element_type=jnp.float32))
    gen_image = image_out.astype(jnp.bfloat16)
    gen_phase = jnp.dot(gen_image, frequencies, preferred_element_type=jnp.float32)
    gen_part, gen_onehot = class_sums(gen_phase, gen_labels, classes, classes / total_gen)
    mean_gap = lax.psum(gen_part - data_part, "dp") - privacy_noise
    match_loss = lax.psum(jnp.sum(mean_gap * mean_gap), "feat") / (2.0 * total_feats)
    gap_rows = jnp.dot(
        gen_onehot, mean_gap.reshape(classes, 2 * feat_dev), precision=lax.Precision.HIGHEST
    ) * (16.0 * classes / total_gen)
    phase_grad = (
        jnp.cos(gen_phase) * gap_rows[:, feat_dev:] - jnp.sin(gen_phase) * gap_rows[:, :feat_dev]
    ).astype(jnp.bfloat16)
    partial_image = jnp.einsum(
        "gf,df->gd", phase_grad, frequencies, preferred_element_type=jnp.float32
    )
    image_grad = lax.psum(partial_image, "feat")
    grad_in, grad_out = generator_grads(
        image_grad, image_out, hidden, pre_hidden, sigmoid_h, latents, gen_out
    )
    grad_in, grad_out = (
        lax.psum_scatter(grad_in, "dp", scatter_dimension=0, tiled=True),
        lax.psum_scatter(grad_out, "dp", scatter_dimension=0, tiled=True),
    )
    return (match_loss, grad_in, grad_out)


def solution(mesh):
    return jax.shard_map(
        per_device,
        mesh=mesh,
        in_specs=(
            P("dp", None),
            P("dp"),
            P(None, "feat"),
            P(None, None, "feat"),
            P("dp", None),
            P("dp"),
            P(),
            P(),
        ),
        out_specs=(P(), P("dp", None), P("dp", None)),
        check_vma=False,
    )
```

profile of v0, /device:TPU:0, one launch (start us, length us, event | category | flops | bytes accessed | tf_op | source)
XLA Modules:
  0.0 356.0 jit_solution(9388458838005756762)
XLA Ops:
  7.2 0.0 all-reduce.3.cloned.1.call-start
  7.2 1.6 fusion.34
  8.8 1.0 copy-done.4
  9.8 4.8 %convolution_tanh_fusion = f32[256,3072]{1,0:T(8,128)S(1)} fusion(bf16[1024,3072]{1,0:T(8,128)(2,1)} %param.15, f32[256,1024]{1,0:T(8,128)S(1)} %fusion.34), kind=kOutput, calls=%fused_computation | convolution fusion | flops 1611923456 | bytes 10485760 | tf_op jit(solution)/shard_map/dot_general | solution.py:38
  14.6 5.3 %fusion.33 = (f32[256,1024]{1,0:T(8,128)S(1)}, f32[256,1024]{1,0:T(8,128)S(1)}) fusion(bf16[3072,1024]{1,0:T(8,128)(2,1)S(1)} %bitcast.19, f32[256,3072]{1,0:T(8,128)S(1)} %convolution_tanh_fusion), kind=kOutput, calls=%fused_computation.41 | convolution fusion | flops 1611399168 | bytes 11534336 | tf_op jit(solution)/shard_map/dot_general | solution.py:40
  20.0 12.3 %fusion.32 = (f32[384,1024]{1,0:T(8,128)S(1)}, f32[384,1024]{1,0:T(8,128)S(1)}) fusion(bf16[384,3072]{1,0:T(8,128)(2,1)S(1)} %copy-done, bf16[3072,1024]{1,0:T(8,128)(2,1)S(1)} %bitcast.19), kind=kOutput, calls=%fused_computation.40 | convolution fusion | flops 2415919104 | bytes 11796480 | tf_op jit(solution)/shard_map/dot_general | solution.py:33
  32.3 0.8 convolution_multiply_fusion.1
  33.1 1.2 fusion.7
  34.3 0.7 sub.22
  35.0 0.2 all-reduce.5.cloned.1.call-start
  35.3 32.9 %all-reduce.3.cloned.1.call-done = f32[10,2,1024]{2,1,0:T(2,128)} async-done(((f32[10,2,1024]{2,1,0:T(2,128)}), f32[10,2,1024]{2,1,0:T(2,128)}) %all-reduce.3.cloned.1.call-update) | async-done | bytes 81936 | tf_op jit(solution)/shard_map/psum | solution.py:42
  68.2 1.7 multiply_reduce_fusion
  70.0 1.0 convolution_multiply_fusion
  71.0 6.4 %fusion.22 = f32[256,3072]{1,0:T(8,128)} fusion(bf16[3072,1024]{1,0:T(8,128)(2,1)} %param.10, f32[256,1024]{1,0:T(8,128)S(1)} %copy-done.3, f32[256,2048]{1,0:T(8,128)S(1)} %convolution_multiply_fusion, f32[256,1024]{1,0:T(8,128)S(1)} %get-tuple-element.13), kind=kOutput, calls=%fused_computation.28 | convolution fusion | flops 1611661312 | bytes 13631488 | tf_op jit(solution)/shard_map/gf,df->gd/dot_general | solution.py:50
  77.5 0.0 reduce-scatter.7.cloned.1.call-start
  77.5 130.2 %all-reduce.5.cloned.1.call-done = f32[256,3072]{1,0:T(8,128)} async-done(((f32[256,3072]{1,0:T(8,128)}), f32[256,3072]{1,0:T(8,128)}) %all-reduce.5.cloned.1.call-update) | async-done | bytes 3145744 | tf_op jit(solution)/shard_map/psum | solution.py:53
  207.7 4.6 %multiply_convert_fusion = bf16[256,3072]{1,0:T(8,128)(2,1)} fusion(f32[256,3072]{1,0:T(8,128)} %all-reduce.5.cloned.1.call-done, f32[256,3072]{1,0:T(8,128)} %copy-done.1), kind=kLoop, calls=%fused_computation.5 | loop fusion | flops 3145728 | bytes 7864320 | tf_op jit(solution)/shard_map/convert_element_type | solution.py:15
  212.3 6.6 %convolution_bitcast_fusion = f32[256,1024]{0,1:T(8,128)} fusion(bf16[256,256]{1,0:T(8,128)(2,1)S(1)} %copy-done.6, bf16[256,3072]{1,0:T(8,128)(2,1)} %multiply_convert_fusion, bf16[1024,3072]{1,0:T(8,128)(2,1)} %param.15, f32[256,1024]{1,0:T(8,128)S(1)} %copy-done.5), kind=kOutput, calls=%fused_computation.17 | convolution fusion | flops 1747189760 | bytes 10092544 | tf_op jit(solution)/shard_map/gz,gh->zh/dot_general | solution.py:21
  218.9 2.6 copy.13
  221.5 0.0 reduce-scatter.5.cloned.1.call-start
  221.5 8.0 %fusion.31 = f32[1024,3072]{1,0:T(8,128)} fusion(bf16[256,3072]{1,0:T(8,128)(2,1)} %multiply_convert_fusion, f32[256,1024]{1,0:T(8,128)S(1)} %copy-done.5), kind=kOutput, calls=%fused_computation.39 | convolution fusion | flops 1611923456 | bytes 15204352 | tf_op jit(solution)/shard_map/gh,gd->hd/dot_general | solution.py:16
  229.6 19.9 %psum.22 = f32[]{:T(128)} all-reduce(f32[]{:T(128)} %get-tuple-element.9), channel_id=1, replica_groups=mesh['dp'=4,'feat'=8] {'feat'}, use_global_device_ids=true, to_apply=%region_2.0 | all-reduce | flops 1 | bytes 8 | tf_op jit(solution)/shard_map/psum | solution.py:43
  250.1 0.0 reduce-scatter.7.cloned.1.call-done
  250.1 98.3 %reduce-scatter.5.cloned.1.call-done = f32[256,3072]{1,0:T(8,128)} async-done(((f32[1024,3072]{1,0:T(8,128)}), f32[256,3072]{1,0:T(8,128)}) %reduce-scatter.5.cloned.1.call-update) | async-done | bytes 3145744 | tf_op jit(solution)/shard_map/reduce_scatter | solution.py:59
  (28 shorter events, 0.2 us)
Async XLA Ops:
  7.2 12.8 %copy-start = (bf16[384,3072]{1,0:T(8,128)(2,1)S(1)}, bf16[384,3072]{1,0:T(8,128)(2,1)}, u32[]{:S(2)}) copy-start(bf16[384,3072]{1,0:T(8,128)(2,1)} %param.8) | copy-start | bytes 7077892
  7.2 61.0 %all-reduce.3.cloned.1.call-start = ((), (), s32[]{:S(2)}) async-start(), calls=%async_computation.2 | async-start | bytes 163840 | tf_op jit(solution)/shard_map/psum | solution.py:42
  7.2 7.4 %slice-start = ((s8[6291456]{0:T(1024)(128)(4,1)}), s8[4194304]{0:T(1024)(128)(4,1)S(1)}, s32[]{:S(2)}) async-start(s8[6291456]{0:T(1024)(128)(4,1)} %bitcast.18), calls=%async_computation.6 | async-start | bytes 8388608
  8.8 1.0 copy-start.4
  9.8 4.8 %slice-start.1 = ((s8[6291456]{0:T(1024)(128)(4,1)}), s8[2097152]{0:T(1024)(128)(4,1)S(1)}, s32[]{:S(2)}) async-start(s8[6291456]{0:T(1024)(128)(4,1)} %bitcast.18), calls=%async_computation.7 | async-start | bytes 4194304
  14.6 5.3 %copy-start.1 = (f32[256,3072]{1,0:T(8,128)}, f32[256,3072]{1,0:T(8,128)S(1)}, u32[]{:S(2)}) copy-start(f32[256,3072]{1,0:T(8,128)S(1)} %convolution_tanh_fusion) | copy-start | bytes 9437188
  20.0 12.3 %copy-start.2 = (f32[256,1024]{1,0:T(8,128)}, f32[256,1024]{1,0:T(8,128)S(1)}, u32[]{:S(2)}) copy-start(f32[256,1024]{1,0:T(8,128)S(1)} %get-tuple-element.14) | copy-start | bytes 3145732
  20.0 12.3 %copy-start.7 = (s32[256]{0:T(256)S(1)}, s32[256]{0:T(256)}, u32[]{:S(2)}) copy-start(s32[256]{0:T(256)} %param.13) | copy-start | bytes 3076
  20.0 13.2 %copy-start.8 = (s32[384]{0:T(512)S(1)}, s32[384]{0:T(512)}, u32[]{:S(2)}) copy-start(s32[384]{0:T(512)} %param.9) | copy-start | bytes 4612
  35.0 172.7 %all-reduce.5.cloned.1.call-start = ((), (), s32[]{:S(2)}) async-start(), calls=%async_computation.3 | async-start | bytes 6291456 | tf_op jit(solution)/shard_map/psum | solution.py:53
  68.2 2.8 copy-start.3
  77.5 134.8 %copy-start.5 = (f32[256,1024]{1,0:T(8,128)S(1)}, f32[256,1024]{1,0:T(8,128)}, u32[]{:S(2)}) copy-start(f32[256,1024]{1,0:T(8,128)} %copy-done.4) | copy-start | bytes 3145732
  77.5 134.8 %copy-start.6 = (bf16[256,256]{1,0:T(8,128)(2,1)S(1)}, bf16[256,256]{1,0:T(8,128)(2,1)}, u32[]{:S(2)}) copy-start(bf16[256,256]{1,0:T(8,128)(2,1)} %param.12) | copy-start | bytes 393220
  77.5 172.6 %reduce-scatter.7.cloned.1.call-start = ((), (), s32[]{:S(2)}) async-start(), calls=%async_computation.5 | async-start | bytes 1310720
  221.5 126.9 %reduce-scatter.5.cloned.1.call-start = ((), (), s32[]{:S(2)}) async-start(), calls=%async_computation.4 | async-start | bytes 15728640 | tf_op jit(solution)/shard_map/reduce_scatter | solution.py:59
Sparse Core Ops, SparseCore 0:
  35.2 32.9 all-reduce.2
  77.6 130.0 all-reduce.4
  221.6 23.8 reduce-scatter.6
  248.5 99.8 reduce-scatter.4
where the time goes:
time: 356 us
  waiting for transfers between devices  261 us (73%)
  matrix products  47.9 us (13%)
  blocking collectives  19.9 us (6%)
  between operations  15.7 us (4%)
  other arithmetic  6.29 us (2%)
  local copies, waits for them, and re-layouts  4.46 us (1%)
    psum x1, waiting for transfers between devices, per_device(): image_grad = lax.psum(partial_image, 'feat')  130 us
    reduce_scatter x1, waiting for transfers between devices, per_device(): lax.psum_scatter(grad_out, 'dp', scatter_dimension=0, tiled=True)  98.3 us
    psum x1, waiting for transfers between devices, per_device(): mean_gap = lax.psum(gen_part - data_part, 'dp') - privacy_noise  32.9 us
    psum x1, blocking collectives, per_device(): lax.psum(jnp.sum(mean_gap * mean_gap), 'feat') / (2.0 * total_feats)  19.9 us
    dot_general x1, matrix products, per_device(): jnp.dot(images, frequencies, preferred_element_type=jnp.float32)  12.3 us
    dot_general x1, matrix products, generator_grads(): jnp.einsum('gh,gd->hd', hidden, out_grad, preferred_element_type=jnp.floa...  8.02 us
  transfers between devices with their start and end apart: 4, of which 3 were waited for; matrix products, arithmetic and copies ran while one was open for 2% of the time, Pallas kernels for 0%

commit v1 on v0

--- a/solution.py
+++ b/solution.py
@@ -50,7 +50,7 @@
     partial_image = jnp.einsum(
         "gf,df->gd", phase_grad, frequencies, preferred_element_type=jnp.float32
     )
-    image_grad = lax.psum(partial_image, "feat")
+    image_grad = jnp.sum(lax.all_gather(partial_image, "feat"), axis=0)
     grad_in, grad_out = generator_grads(
         image_grad, image_out, hidden, pre_hidden, sigmoid_h, latents, gen_out
     )

time: 356 us -> 719 us (2.02)
  waiting for transfers between devices: 261 us -> 614 us
  other arithmetic: 6.29 us -> 16.6 us
    all_gather x0 -> x1, waiting for transfers between devices: none -> 482 us  [per_device(): image_grad = jnp.sum(lax.all_gather(partial_image, 'feat'), axis=0)]
    psum x1 -> x0, waiting for transfers between devices: 130 us -> none  [per_device(): image_grad = lax.psum(partial_image, 'feat')]
    reduce_sum x0 -> x1, other arithmetic: none -> 11.5 us  [per_device(): image_grad = jnp.sum(lax.all_gather(partial_image, 'feat'), axis=0)]
  transfers between devices with their start and end apart: 4 -> 4, of which waited for: 3 -> 3; matrix products, arithmetic and copies ran while one was open for 2% -> 1% of each run, Pallas kernels for 0% -> 0%
where the time goes in v1:
time: 719 us; the launch traced here: 718 us
  waiting for transfers between devices  614 us (85%)
  matrix products  45.8 us (6%)
  blocking collectives  20.8 us (3%)
  other arithmetic  16.6 us (2%)
  between operations  15.8 us (2%)
    all_gather x1, waiting for transfers between devices, per_device(): image_grad = jnp.sum(lax.all_gather(partial_image, 'feat'), axis=0)  482 us
    reduce_scatter x1, waiting for transfers between devices, per_device(): lax.psum_scatter(grad_out, 'dp', scatter_dimension=0, tiled=True)  99.5 us
    psum x1, waiting for transfers between devices, per_device(): mean_gap = lax.psum(gen_part - data_part, 'dp') - privacy_noise  32.9 us
    psum x1, blocking collectives, per_device(): lax.psum(jnp.sum(mean_gap * mean_gap), 'feat') / (2.0 * total_feats)  20.8 us
  transfers between devices with their start and end apart: 4, of which 3 were waited for; matrix products, arithmetic and copies ran while one was open for 1% of the time, Pallas kernels for 0%

profile of v1, /device:TPU:0, one launch (start us, length us, event | category | flops | bytes accessed | tf_op | source)
XLA Modules:
  0.0 718.2 jit_solution(788916686689775193)
XLA Ops:
  7.2 0.0 all-reduce.2.cloned.1.call-start
  7.2 1.6 fusion.34
  8.8 1.0 copy-done.5
  9.8 4.8 convolution_tanh_fusion
  14.6 5.3 fusion.33
  20.0 12.3 %fusion.32 = (f32[384,1024]{1,0:T(8,128)S(1)}, f32[384,1024]{1,0:T(8,128)S(1)}) fusion(bf16[384,3072]{1,0:T(8,128)(2,1)S(1)} %copy-done, bf16[3072,1024]{1,0:T(8,128)(2,1)S(1)} %bitcast.20), kind=kOutput, calls=%fused_computation.40 | convolution fusion | flops 2415919104 | bytes 11796480 | tf_op jit(solution)/shard_map/dot_general | solution.py:33
  32.3 0.8 convolution_multiply_fusion.1
  33.2 1.2 fusion.7
  34.3 0.7 sub.22
  35.1 0.2 all-gather.3.cloned.1.call-start
  35.3 32.9 %all-reduce.2.cloned.1.call-done = f32[10,2,1024]{2,1,0:T(2,128)} async-done(((f32[10,2,1024]{2,1,0:T(2,128)}), f32[10,2,1024]{2,1,0:T(2,128)}) %all-reduce.2.cloned.1.call-update) | async-done | bytes 81936 | tf_op jit(solution)/shard_map/psum | solution.py:42
  68.2 1.6 multiply_reduce_fusion
  69.9 1.0 convolution_multiply_fusion
  70.9 6.4 fusion.22
  77.4 0.0 reduce-scatter.7.cloned.1.call-start
  77.4 481.8 %all-gather.3.cloned.1.call-done = f32[2048,3072]{1,0:T(8,128)} async-done(((f32[256,3072]{1,0:T(8,128)}), f32[2048,3072]{1,0:T(8,128)}) %all-gather.3.cloned.1.call-update) | async-done | bytes 25165840 | tf_op jit(solution)/shard_map/all_gather | solution.py:53
  559.2 11.5 %reduce_sum.19 = f32[256,3072]{1,0:T(8,128)} reduce(f32[8,256,3072]{2,1,0:T(8,128)} %bitcast.21, f32[]{:T(128)} %constant.3.clone.1), dimensions={0}, to_apply=%region_3.0 | reduce | flops 5505024 | bytes 28311556 | tf_op jit(solution)/shard_map/reduce_sum | solution.py:53
  570.7 3.5 multiply_convert_fusion
  574.3 6.1 convolution_bitcast_fusion
  580.3 2.6 copy.13
  583.0 0.0 reduce-scatter.5.cloned.1.call-start
  583.0 6.4 fusion.31
  589.5 20.8 %psum.15 = f32[]{:T(128)} all-reduce(f32[]{:T(128)} %get-tuple-element.9), channel_id=1, replica_groups=mesh['dp'=4,'feat'=8] {'feat'}, use_global_device_ids=true, to_apply=%region_2.0 | all-reduce | flops 1 | bytes 8 | tf_op jit(solution)/shard_map/psum | solution.py:43
  611.0 99.5 %reduce-scatter.5.cloned.1.call-done = f32[256,3072]{1,0:T(8,128)} async-done(((f32[1024,3072]{1,0:T(8,128)}), f32[256,3072]{1,0:T(8,128)}) %reduce-scatter.5.cloned.1.call-update) | async-done | bytes 3145744 | tf_op jit(solution)/shard_map/reduce_scatter | solution.py:59
  (33 shorter events, 0.2 us)
Async XLA Ops:
  7.2 12.8 %copy-start = (bf16[384,3072]{1,0:T(8,128)(2,1)S(1)}, bf16[384,3072]{1,0:T(8,128)(2,1)}, u32[]{:S(2)}) copy-start(bf16[384,3072]{1,0:T(8,128)(2,1)} %param.8) | copy-start | bytes 7077892
  7.2 61.0 %all-reduce.2.cloned.1.call-start = ((), (), s32[]{:S(2)}) async-start(), calls=%async_computation.2 | async-start | bytes 163840 | tf_op jit(solution)/shard_map/psum | solution.py:42
  7.2 7.4 %slice-start = ((s8[6291456]{0:T(1024)(128)(4,1)}), s8[4194304]{0:T(1024)(128)(4,1)S(1)}, s32[]{:S(2)}) async-start(s8[6291456]{0:T(1024)(128)(4,1)} %bitcast.19), calls=%async_computation.6 | async-start | bytes 8388608
  8.8 1.0 copy-start.5
  9.8 4.8 slice-start.1
  14.6 5.3 copy-start.2
  19.9 12.3 %copy-start.3 = (f32[256,1024]{1,0:T(8,128)}, f32[256,1024]{1,0:T(8,128)S(1)}, u32[]{:S(2)}) copy-start(f32[256,1024]{1,0:T(8,128)S(1)} %get-tuple-element.14) | copy-start | bytes 3145732
  20.0 12.3 %copy-start.9 = (s32[256]{0:T(256)S(1)}, s32[256]{0:T(256)}, u32[]{:S(2)}) copy-start(s32[256]{0:T(256)} %param.13) | copy-start | bytes 3076
  20.0 13.2 %copy-start.10 = (s32[384]{0:T(512)S(1)}, s32[384]{0:T(512)}, u32[]{:S(2)}) copy-start(s32[384]{0:T(512)} %param.9) | copy-start | bytes 4612
  32.3 35.9 %copy-start.8 = (f32[10,2,1024]{2,1,0:T(2,128)S(1)}, f32[10,2,1024]{2,1,0:T(2,128)}, u32[]{:S(2)}) copy-start(f32[10,2,1024]{2,1,0:T(2,128)} %param.11) | copy-start | bytes 245764
  33.1 37.8 %copy-start.4 = (f32[256,1024]{1,0:T(8,128)S(1)}, f32[256,1024]{1,0:T(8,128)}, u32[]{:S(2)}) copy-start(f32[256,1024]{1,0:T(8,128)} %copy-done.3) | copy-start | bytes 3145732
  35.1 524.2 %all-gather.3.cloned.1.call-start = ((), (), s32[]{:S(2)}) async-start(), calls=%async_computation.4 | async-start | bytes 28311552 | tf_op jit(solution)/shard_map/all_gather | solution.py:53
  77.4 533.6 %reduce-scatter.7.cloned.1.call-start = ((), (), s32[]{:S(2)}) async-start(), calls=%async_computation.5 | async-start | bytes 1310720
  570.7 3.5 copy-start.6
  570.7 3.5 copy-start.7
  583.0 127.6 %reduce-scatter.5.cloned.1.call-start = ((), (), s32[]{:S(2)}) async-start(), calls=%async_computation.3 | async-start | bytes 15728640 | tf_op jit(solution)/shard_map/reduce_scatter | solution.py:59
  589.5 121.1 %copy-start.1 = (bf16[384,3072]{1,0:T(8,128)(2,1)S(1)}, bf16[384,3072]{1,0:T(8,128)(2,1)}, u32[]{:S(2)}) copy-start(bf16[384,3072]{1,0:T(8,128)(2,1)} %param.8) | copy-start | bytes 7077892
Sparse Core Ops, SparseCore 0:
  35.2 32.9 all-reduce.1
  77.5 481.7 all-gather.2
  583.1 24.7 reduce-scatter.6
  610.9 99.6 reduce-scatter.4
